TPU v7x, 32 devices: a whole 2x2x4 slice. The times are simulated.
32 devices in a mesh: rep: 4 (over x, core), row: 4 (over z), col: 2 (over y).
Axes of the slice: x: 2, y: 2, z: 4, core: 2. Of those that a mesh axis runs over, the one named last changes fastest.
Arguments:
- inputs: bfloat16 [4, 128, 6144], P('rep', 'col', 'row'), may hold values from -6 to 6
- w_in: bfloat16 [6144, 24576], P('row', ('rep', 'col')), may hold values from -0.078125 to 0.078125
- w_out: bfloat16 [24576, 6144], P(('rep', 'col'), 'row'), may hold values from -0.0390625 to 0.0390625
- cotangent: bfloat16 [4, 128, 6144], P('rep', 'col', 'row'), may hold values from -1536 to 1536
- counts: int32 [4], replicated, may hold values from 0 to 4, as said below
Outputs:
- block_output: bfloat16 [4, 128, 6144], P('rep', 'col', 'row')
- input_grad: bfloat16 [4, 128, 6144], P('rep', 'col', 'row')
- w_in_grad: float32 [6144, 24576], P('row', ('rep', 'col'))
- w_out_grad: float32 [24576, 6144], P(('rep', 'col'), 'row')
Inputs may be any that keep to these rules, and one draw needn't show every extreme that they name: Replica r completed its first counts[r] micro-batches; at least one replica completed all 4.
All inputs are finite; a program needn't handle non-finite values.
Results may differ from a plain program's by a relative error of at most 0.015.
Values may be sent and summed in bfloat16 or wider, within the bound.
A program may use at most 192 MiB of HBM per device.

v0:
```python
import jax
import jax.numpy as jnp
from jax import lax
from jax.sharding import PartitionSpec as P

MBT = 32
root_coef = 0.7978845608028654
cubic_coef = 0.044715


def gelu_tanh(values):
    inner = root_coef * (values + cubic_coef * values * values * values)
    return 0.5 * values * (1.0 + jnp.tanh(inner))


def gelu_slope(values):
    inner = root_coef * (values + cubic_coef * values * values * values)
    tangent = jnp.tanh(inner)
    return 0.5 * (1.0 + tangent) + 0.5 * values * (1.0 - tangent * tangent) * root_coef * (
        1.0 + 3.0 * cubic_coef * values * values
    )


def right_product(left, right):
    return lax.dot_general(
        left, right, (((1,), (1,)), ((), ())), preferred_element_type=jnp.float32
    )


def first_product(left, right):
    return lax.dot_general(
        left, right, (((0,), (0,)), ((), ())), preferred_element_type=jnp.float32
    )


def body(inputs, w_in, w_out, cotangent, counts):
    rows_local = inputs.shape[1]
    width_local = inputs.shape[2]
    tokens_local = inputs.reshape(rows_local, width_local)
    replicas = lax.axis_size("rep")
    replica_index = lax.axis_index("rep")
    column_index = lax.axis_index("col")
    own_count = jnp.sum(jnp.where(jnp.arange(replicas) == replica_index, counts, 0))
    token_total = (MBT * jnp.sum(counts)).astype(jnp.float32)
    positions = column_index * rows_local + jnp.arange(rows_local, dtype=jnp.int32)
    kept_mask = (positions // MBT < own_count).astype(jnp.float32)
    scaled = (
        cotangent.reshape(rows_local, width_local).astype(jnp.float32)
        * kept_mask[:, None]
        / token_total
    ).astype(jnp.bfloat16)
    tokens_all, scaled_all = (
        lax.all_gather(tokens_local, "col", axis=0, tiled=True),
        lax.all_gather(scaled, "col", axis=0, tiled=True),
    )
    inner_cols = lax.all_gather(w_in, "rep", axis=1, tiled=True)
    outer_rows = lax.all_gather(w_out, "rep", axis=0, tiled=True)
    partial_hidden = jnp.dot(tokens_all, inner_cols, preferred_element_type=jnp.float32)
    hidden = lax.psum_scatter(
        partial_hidden.astype(jnp.bfloat16), "row", scatter_dimension=0, tiled=True
    ).astype(jnp.float32)
    active_share = gelu_tanh(hidden).astype(jnp.bfloat16)
    activated = lax.all_gather(active_share, "row", axis=0, tiled=True)
    output_terms = jnp.dot(activated, outer_rows, preferred_element_type=jnp.float32)
    output_local = lax.psum_scatter(
        output_terms.astype(jnp.bfloat16), "col", scatter_dimension=0, tiled=True
    ).astype(jnp.float32)
    block_output = (tokens_local.astype(jnp.float32) + output_local).astype(jnp.bfloat16)
    slope_terms = right_product(scaled_all, outer_rows)
    slope_sum = lax.psum_scatter(
        slope_terms.astype(jnp.bfloat16), "row", scatter_dimension=0, tiled=True
    ).astype(jnp.float32)
    grad_share = (slope_sum * gelu_slope(hidden)).astype(jnp.bfloat16)
    hidden_grad = lax.all_gather(grad_share, "row", axis=0, tiled=True)
    back_terms = right_product(hidden_grad, inner_cols)
    back_local = lax.psum_scatter(
        back_terms.astype(jnp.bfloat16), "col", scatter_dimension=0, tiled=True
    ).astype(jnp.float32)
    input_grad = (scaled.astype(jnp.float32) + back_local).astype(jnp.bfloat16)
    token_reps, scaled_reps = (
        lax.all_gather(tokens_all, "rep", axis=0, tiled=True),
        lax.all_gather(scaled_all, "rep", axis=0, tiled=True),
    )
    hidden_reps, active_reps = (
        lax.all_to_all(hidden_grad, "rep", split_axis=1, concat_axis=0, tiled=True),
        lax.all_to_all(activated, "rep", split_axis=1, concat_axis=0, tiled=True),
    )
    w_in_grad = first_product(token_reps, hidden_reps)
    w_out_grad = first_product(active_reps, scaled_reps)
    return (
        block_output.reshape(1, rows_local, width_local),
        input_grad.reshape(1, rows_local, width_local),
        w_in_grad,
        w_out_grad,
    )


def solution(mesh):
    placed = (
        P("rep", "col", "row"),
        P("row", ("rep", "col")),
        P(("rep", "col"), "row"),
        P("rep", "col", "row"),
        P(),
    )
    return jax.shard_map(
        body,
        mesh=mesh,
        in_specs=placed,
        out_specs=(
            P("rep", "col", "row"),
            P("rep", "col", "row"),
            P("row", ("rep", "col")),
            P(("rep", "col"), "row"),
        ),
        check_vma=False,
    )
```

profile of v0, /device:TPU:0, one launch (start us, length us, event | category | flops | bytes accessed | tf_op | source)
XLA Modules:
  0.0 861.8 jit_solution(15907317632032920485)
XLA Ops:
  8.8 8.5 all-gather
  17.4 222.1 %all-gather.9.cloned.1.call-done = bf16[1536,12288]{1,0:T(8,128)(2,1)} async-done(((bf16[1536,3072]{1,0:T(8,128)(2,1)}), bf16[1536,12288]{1,0:T(8,128)(2,1)}) %all-gather.9.cloned.1.call-update) | async-done | bytes 37748752 | tf_op jit(solution)/shard_map/all_gather | solution.py:56
  239.5 20.2 %convolution_convert_fusion.1 = bf16[128,12288]{1,0:T(8,128)(2,1)} fusion(bf16[1536,12288]{1,0:T(8,128)(2,1)} %all-gather.9.cloned.1.call-done, bf16[1,128,1536]{2,1,0:T(8,128)(2,1)S(1)} %all-gather), kind=kOutput, calls=%fused_computation.1 | convolution fusion | flops 4833411072 | bytes 41287680 | tf_op jit(solution)/shard_map/dot_general | solution.py:58
  262.4 7.7 all_gather.28
  270.1 198.2 %all-gather.13.cloned.1.call-done = bf16[12288,1536]{1,0:T(8,128)(2,1)} async-done(((bf16[3072,1536]{1,0:T(8,128)(2,1)}), bf16[12288,1536]{1,0:T(8,128)(2,1)}) %all-gather.13.cloned.1.call-update) | async-done | bytes 37748752 | tf_op jit(solution)/shard_map/all_gather | solution.py:57
  468.3 19.7 %convolution_convert_fusion = bf16[128,12288]{1,0:T(8,128)(2,1)} fusion(bf16[128,1536]{1,0:T(8,128)(2,1)S(1)} %all_gather.28, bf16[12288,1536]{1,0:T(8,128)(2,1)} %all-gather.13.cloned.1.call-done), kind=kOutput, calls=%fused_computation | convolution fusion | flops 4833411072 | bytes 41287680 | tf_op jit(solution)/shard_map/dot_general | solution.py:25
  488.1 43.5 %reduce-scatter.5.cloned.1.call-done = bf16[32,12288]{1,0:T(8,128)(2,1)} async-done(((bf16[128,12288]{1,0:T(8,128)(2,1)}), bf16[32,12288]{1,0:T(8,128)(2,1)}) %reduce-scatter.5.cloned.1.call-update) | async-done | bytes 786448 | tf_op jit(solution)/shard_map/reduce_scatter | solution.py:59
  531.6 63.0 %reduce-scatter.9.cloned.1.call-done = bf16[32,12288]{1,0:T(8,128)(2,1)} async-done(((bf16[128,12288]{1,0:T(8,128)(2,1)}), bf16[32,12288]{1,0:T(8,128)(2,1)}) %reduce-scatter.9.cloned.1.call-update) | async-done | bytes 786448 | tf_op jit(solution)/shard_map/reduce_scatter | solution.py:70
  594.6 3.7 fusion.7
  599.0 62.9 %all-gather.11.cloned.1.call-done = bf16[128,12288]{1,0:T(8,128)(2,1)} async-done(((bf16[32,12288]{1,0:T(8,128)(2,1)}), bf16[128,12288]{1,0:T(8,128)(2,1)}) %all-gather.11.cloned.1.call-update) | async-done | bytes 3145744 | tf_op jit(solution)/shard_map/all_gather | solution.py:63
  661.9 16.8 %convolution_convert_fusion.3 = bf16[128,1536]{1,0:T(8,128)(2,1)} fusion(bf16[128,12288]{1,0:T(8,128)(2,1)} %all-gather.11.cloned.1.call-done, bf16[12288,1536]{1,0:T(8,128)(2,1)} %all-gather.13.cloned.1.call-done), kind=kOutput, calls=%fused_computation.13 | convolution fusion | flops 4832034816 | bytes 41287680 | tf_op jit(solution)/shard_map/dot_general | solution.py:64
  678.9 47.1 %all-gather.15.cloned.1.call-done = bf16[128,12288]{1,0:T(8,128)(2,1)} async-done(((bf16[32,12288]{1,0:T(8,128)(2,1)}), bf16[128,12288]{1,0:T(8,128)(2,1)}) %all-gather.15.cloned.1.call-update) | async-done | bytes 3145744 | tf_op jit(solution)/shard_map/all_gather | solution.py:74
  726.0 23.0 %convolution_convert_fusion.2 = bf16[128,1536]{1,0:T(8,128)(2,1)} fusion(bf16[128,12288]{1,0:T(8,128)(2,1)} %all-gather.15.cloned.1.call-done, bf16[1536,12288]{1,0:T(8,128)(2,1)} %all-gather.9.cloned.1.call-done), kind=kOutput, calls=%fused_computation.12 | convolution fusion | flops 4832034816 | bytes 41287680 | tf_op jit(solution)/shard_map/dot_general | solution.py:25
  749.8 1.9 copy.18
  751.7 4.9 all-to-all-start
  757.2 1.9 copy.17
  759.2 42.9 %all-to-all-done = bf16[128,4,3072]{2,0,1:T(8,128)(2,1)} async-done(((bf16[128,4,3072]{2,0,1:T(8,128)(2,1)}), bf16[128,4,3072]{2,0,1:T(8,128)(2,1)}, u32[]{:S(2)}, u32[]{:S(2)}) %all-to-all-start) | async-done | bytes 3145760 | tf_op jit(solution)/shard_map/all_to_all | solution.py:85
  802.0 3.8 all-to-all-start.1
  805.9 1.7 fusion.17
  807.6 1.7 fusion.16
  809.3 11.4 %convolution_bitcast_fusion = f32[1536,3072]{0,1:T(8,128)} fusion(bf16[512,3072]{1,0:T(8,128)(2,1)} %bitcast.6, bf16[1,512,1536]{2,1,0:T(8,128)(2,1)} %all-gather.19.cloned.1.call-done), kind=kOutput, calls=%fused_computation.2 | convolution fusion | flops 4831838208 | bytes 23592960 | tf_op jit(solution)/shard_map/dot_general | solution.py:31
  820.7 18.6 %copy.12 = f32[1536,3072]{1,0:T(8,128)} copy(f32[1536,3072]{0,1:T(8,128)} %convolution_bitcast_fusion) | data formatting | bytes 37748736
  839.3 4.7 all-to-all-done.1
  844.1 10.9 %fusion.19 = f32[3072,1536]{1,0:T(8,128)} fusion(bf16[512,3072]{1,0:T(8,128)(2,1)S(1)} %bitcast.48, bf16[512,1536]{1,0:T(8,128)(2,1)} %all-gather.17.cloned.1.call-done), kind=kOutput, calls=%fused_computation.42 | convolution fusion | flops 4831838208 | bytes 23592960 | tf_op jit(solution)/shard_map/dot_general | solution.py:31
  (45 shorter events, 6.0 us)
Async XLA Ops:
  7.2 232.3 %all-gather.9.cloned.1.call-start = ((), (), s32[]{:S(2)}) async-start(), calls=%async_computation.6 | async-start | bytes 47185920 | tf_op jit(solution)/shard_map/all_gather | solution.py:56
  7.9 0.9 copy-start.6
  7.9 460.3 %all-gather.13.cloned.1.call-start = ((), (), s32[]{:S(2)}) async-start(), calls=%async_computation.9 | async-start | bytes 47185920 | tf_op jit(solution)/shard_map/all_gather | solution.py:57
  8.7 522.9 %reduce-scatter.5.cloned.1.call-start = ((), (), s32[]{:S(2)}) async-start(), calls=%async_computation.7 | async-start | bytes 3932160 | tf_op jit(solution)/shard_map/reduce_scatter | solution.py:59
  17.4 242.3 %copy-start.2 = (bf16[1,128,1536]{2,1,0:T(8,128)(2,1)}, bf16[1,128,1536]{2,1,0:T(8,128)(2,1)S(1)}, u32[]{:S(2)}) copy-start(bf16[1,128,1536]{2,1,0:T(8,128)(2,1)S(1)} %all-gather) | copy-start | bytes 1179652
  259.6 0.7 copy-start.8
  259.6 2.6 copy-start.4
  259.7 335.0 %reduce-scatter.9.cloned.1.call-start = ((), (), s32[]{:S(2)}) async-start(), calls=%async_computation.11 | async-start | bytes 3932160 | tf_op jit(solution)/shard_map/reduce_scatter | solution.py:70
  270.1 217.9 %copy-start.3 = (bf16[128,1536]{1,0:T(8,128)(2,1)}, bf16[128,1536]{1,0:T(8,128)(2,1)S(1)}, u32[]{:S(2)}) copy-start(bf16[128,1536]{1,0:T(8,128)(2,1)S(1)} %all_gather.28) | copy-start | bytes 1179652
  488.0 173.8 %all-gather.11.cloned.1.call-start = ((), (), s32[]{:S(2)}) async-start(), calls=%async_computation.8 | async-start | bytes 3932160 | tf_op jit(solution)/shard_map/all_gather | solution.py:63
  598.3 127.6 %all-gather.15.cloned.1.call-start = ((), (), s32[]{:S(2)}) async-start(), calls=%async_computation.12 | async-start | bytes 3932160 | tf_op jit(solution)/shard_map/all_gather | solution.py:74
  598.9 207.0 %reduce-scatter.7.cloned.1.call-start = ((), (), s32[]{:S(2)}) async-start(), calls=%async_computation.10 | async-start | bytes 589824 | tf_op jit(solution)/shard_map/reduce_scatter | solution.py:65
  678.7 128.9 %reduce-scatter.11.cloned.1.call-start = ((), (), s32[]{:S(2)}) async-start(), calls=%async_computation.13 | async-start | bytes 589824 | tf_op jit(solution)/shard_map/reduce_scatter | solution.py:76
  726.0 23.8 %copy-start = (bf16[128,12288]{1,0:T(8,128)(2,1)S(1)}, bf16[128,12288]{1,0:T(8,128)(2,1)}, u32[]{:S(2)}) copy-start(bf16[128,12288]{1,0:T(8,128)(2,1)} %all-gather.15.cloned.1.call-done) | copy-start | bytes 9437188
  749.0 60.3 %all-gather.19.cloned.1.call-start = ((), (), s32[]{:S(2)}) async-start(), calls=%async_computation.15 | async-start | bytes 1966080 | tf_op jit(solution)/shard_map/all_gather | solution.py:81
  751.7 5.5 copy-start.1
  751.7 50.3 %all-to-all-start = ((bf16[128,4,3072]{2,0,1:T(8,128)(2,1)}), bf16[128,4,3072]{2,0,1:T(8,128)(2,1)}, u32[]{:S(2)}, u32[]{:S(2)}) async-start(bf16[128,4,3072]{2,0,1:T(8,128)(2,1)} %bitcast.47), calls=%async_computation.4 | async-start | bytes 6291456 | tf_op jit(solution)/shard_map/all_to_all | solution.py:85
  756.6 82.7 %all-gather.17.cloned.1.call-start = ((), (), s32[]{:S(2)}) async-start(), calls=%async_computation.14 | async-start | bytes 1966080 | tf_op jit(solution)/shard_map/all_gather | solution.py:82
  802.0 3.9 copy-start.7
  802.0 5.5 copy-start.5
  802.0 42.0 %all-to-all-start.1 = ((bf16[128,4,3072]{2,0,1:T(8,128)(2,1)}), bf16[128,4,3072]{2,0,1:T(8,128)(2,1)S(1)}, u32[]{:S(2)}, u32[]{:S(2)}) async-start(bf16[128,4,3072]{2,0,1:T(8,128)(2,1)} %bitcast.46), calls=%async_computation.5 | async-start | bytes 6291456 | tf_op jit(solution)/shard_map/all_to_all | solution.py:86
Sparse Core Ops, SparseCore 0:
  9.5 229.8 all-gather.8
  241.0 227.1 all-gather.12
  471.1 60.4 reduce-scatter.4
  534.3 60.2 reduce-scatter.8
  598.5 63.3 all-gather.10
  663.9 62.0 all-gather.14
  728.8 11.8 reduce-scatter.6
  749.1 11.8 reduce-scatter.10
  762.6 28.1 all-gather.18
  792.2 21.0 all-gather.16
where the time goes:
time: 863 us; the launch traced here: 862 us
  waiting for transfers between devices  688 us (80%)
  matrix products  102 us (12%)
  local copies, waits for them, and re-layouts  23.2 us (3%)
  blocking collectives  16.2 us (2%)
  between operations  14.9 us (2%)
  starting transfers between devices  9.32 us (1%)
    all_gather x1, waiting for transfers between devices, body(): inner_cols = lax.all_gather(w_in, 'rep', axis=1, tiled=True)  222 us
    all_gather x1, waiting for transfers between devices, body(): outer_rows = lax.all_gather(w_out, 'rep', axis=0, tiled=True)  198 us
    reduce_scatter x1, waiting for transfers between devices, body(): lax.psum_scatter(slope_terms.astype(jnp.bfloat16), 'row', scatter_dimensi...  63 us
    all_gather x1, waiting for transfers between devices, body(): activated = lax.all_gather(active_share, 'row', axis=0, tiled=True)  62.9 us
    all_gather x1, waiting for transfers between devices, body(): hidden_grad = lax.all_gather(grad_share, 'row', axis=0, tiled=True)  47.1 us
    reduce_scatter x1, waiting for transfers between devices, body(): lax.psum_scatter(partial_hidden.astype(jnp.bfloat16), 'row', scatter_dime...  43.5 us
    all_to_all x1, waiting for transfers between devices, body(): lax.all_to_all(hidden_grad, 'rep', split_axis=1, concat_axis=0, tiled=True)  42.9 us
    dot_general x2, matrix products, right_product(): lax.dot_general(left, right, (((1,), (1,)), ((), ())), preferred_element_...  42.8 us
  transfers between devices with their start and end apart: 12, of which 8 were waited for; matrix products, arithmetic and copies ran while one was open for 14% of the time, Pallas kernels for 0%

commit v1 on v0

--- a/solution.py
+++ b/solution.py
@@ -71,7 +71,25 @@
         slope_terms.astype(jnp.bfloat16), "row", scatter_dimension=0, tiled=True
     ).astype(jnp.float32)
     grad_share = (slope_sum * gelu_slope(hidden)).astype(jnp.bfloat16)
-    hidden_grad = lax.all_gather(grad_share, "row", axis=0, tiled=True)
+    peers, index, rows = (lax.axis_size("row"), lax.axis_index("row"), grad_share.shape[0])
+    route = [(i, (i + 1) % peers) for i in range(peers)]
+    behind = [(i, (i - 1) % peers) for i in range(peers)]
+    hidden_grad = jnp.zeros(
+        (*grad_share.shape[:0], peers * rows, *grad_share.shape[0 + 1 :]), grad_share.dtype
+    )
+    hidden_grad = lax.dynamic_update_slice_in_dim(hidden_grad, grad_share, index * rows, axis=0)
+    from_left = from_right = grad_share
+    halfway = peers // 2
+    for step in range(1, halfway + 1):
+        from_left = lax.ppermute(from_left, "row", route)
+        hidden_grad = lax.dynamic_update_slice_in_dim(
+            hidden_grad, from_left, (index - step) % peers * rows, axis=0
+        )
+        if step < peers - halfway:
+            from_right = lax.ppermute(from_right, "row", behind)
+            hidden_grad = lax.dynamic_update_slice_in_dim(
+                hidden_grad, from_right, (index + step) % peers * rows, axis=0
+            )
     back_terms = right_product(hidden_grad, inner_cols)
     back_local = lax.psum_scatter(
         back_terms.astype(jnp.bfloat16), "col", scatter_dimension=0, tiled=True

time: 863 us -> 933 us (1.081)
  local copies, waits for them, and re-layouts: 23.2 us -> 162 us
  waiting for transfers between devices: 688 us -> 592 us
  starting transfers between devices: 9.32 us -> 39.1 us
    dynamic_update_slice x0 -> x4, local copies, waits for them, and re-layouts: none -> 122 us  [the longest x2 63.7 us: body(): lax.dynamic_update_slice_in_dim(hidden_grad, from_left, (index - step) %...]
    all_gather x1, waiting for transfers between devices: 62.9 us -> 0.02 us  [body(): activated = lax.all_gather(active_share, 'row', axis=0, tiled=True)]
    all_gather x1 -> x0, waiting for transfers between devices: 47.1 us -> none  [body(): hidden_grad = lax.all_gather(grad_share, 'row', axis=0, tiled=True)]
    ppermute x0 -> x3, starting transfers between devices: none -> 30 us  [the longest x2 27.1 us: body(): from_left = lax.ppermute(from_left, 'row', route)]
    ppermute x0 -> x3, waiting for transfers between devices: none -> 28.7 us  [the longest x2 28.7 us: body(): from_left = lax.ppermute(from_left, 'row', route)]
    all_to_all x1, waiting for transfers between devices: 42.9 us -> 26.2 us  [body(): lax.all_to_all(hidden_grad, 'rep', split_axis=1, concat_axis=0, tiled=True)]
    unnamed x19 -> x17, local copies, waits for them, and re-layouts: 19.4 us -> 19.4 us
  transfers between devices with their start and end apart: 12 -> 14, of which waited for: 8 -> 7; matrix products, arithmetic and copies ran while one was open for 14% -> 27% of each run, Pallas kernels for 0% -> 0%
where the time goes in v1:
time: 933 us; the launch traced here: 929 us
  waiting for transfers between devices  592 us (63%)
  local copies, waits for them, and re-layouts  162 us (17%)
  matrix products  97.8 us (10%)
  starting transfers between devices  39.1 us (4%)
  blocking collectives  16.2 us (2%)
  between operations  14.7 us (2%)
    all_gather x1, waiting for transfers between devices, body(): inner_cols = lax.all_gather(w_in, 'rep', axis=1, tiled=True)  222 us
    all_gather x1, waiting for transfers between devices, body(): outer_rows = lax.all_gather(w_out, 'rep', axis=0, tiled=True)  198 us
    dynamic_update_slice x2, local copies, waits for them, and re-layouts, body(): lax.dynamic_update_slice_in_dim(hidden_grad, from_left, (index - step) %...  63.7 us
    reduce_scatter x1, waiting for transfers between devices, body(): lax.psum_scatter(slope_terms.astype(jnp.bfloat16), 'row', scatter_dimensi...  63.1 us
    reduce_scatter x1, waiting for transfers between devices, body(): lax.psum_scatter(partial_hidden.astype(jnp.bfloat16), 'row', scatter_dime...  43.5 us
    dot_general x2, matrix products, right_product(): lax.dot_general(left, right, (((1,), (1,)), ((), ())), preferred_element_...  38.9 us
    dynamic_update_slice x1, local copies, waits for them, and re-layouts, body(): lax.dynamic_update_slice_in_dim(hidden_grad, from_right, (index + step) %...  31.8 us
    ppermute x2, waiting for transfers between devices, body(): from_left = lax.ppermute(from_left, 'row', route)  28.7 us
  transfers between devices with their start and end apart: 14, of which 7 were waited for; matrix products, arithmetic and copies ran while one was open for 27% of the time, Pallas kernels for 0%

profile of v1, /device:TPU:0, one launch (start us, length us, event | category | flops | bytes accessed | tf_op | source)
XLA Modules:
  0.0 929.4 jit_solution(12833547399066021182)
XLA Ops:
  8.8 8.5 all-gather
  17.4 222.1 %all-gather.8.cloned.1.call-done = bf16[1536,12288]{1,0:T(8,128)(2,1)} async-done(((bf16[1536,3072]{1,0:T(8,128)(2,1)}), bf16[1536,12288]{1,0:T(8,128)(2,1)}) %all-gather.8.cloned.1.call-update) | async-done | bytes 37748752 | tf_op jit(solution)/shard_map/all_gather | solution.py:56
  239.5 20.2 %convolution_convert_fusion.1 = bf16[128,12288]{1,0:T(8,128)(2,1)} fusion(bf16[1536,12288]{1,0:T(8,128)(2,1)} %all-gather.8.cloned.1.call-done, bf16[1,128,1536]{2,1,0:T(8,128)(2,1)S(1)} %all-gather), kind=kOutput, calls=%fused_computation.1 | convolution fusion | flops 4833411072 | bytes 41287680 | tf_op jit(solution)/shard_map/dot_general | solution.py:58
  262.4 7.7 all_gather.25
  270.1 198.2 %all-gather.12.cloned.1.call-done = bf16[12288,1536]{1,0:T(8,128)(2,1)} async-done(((bf16[3072,1536]{1,0:T(8,128)(2,1)}), bf16[12288,1536]{1,0:T(8,128)(2,1)}) %all-gather.12.cloned.1.call-update) | async-done | bytes 37748752 | tf_op jit(solution)/shard_map/all_gather | solution.py:57
  468.3 19.8 %convolution_convert_fusion = bf16[128,12288]{1,0:T(8,128)(2,1)} fusion(bf16[128,1536]{1,0:T(8,128)(2,1)S(1)} %all_gather.25, bf16[12288,1536]{1,0:T(8,128)(2,1)} %all-gather.12.cloned.1.call-done), kind=kOutput, calls=%fused_computation | convolution fusion | flops 4833411072 | bytes 41287680 | tf_op jit(solution)/shard_map/dot_general | solution.py:25
  488.1 43.5 %reduce-scatter.5.cloned.1.call-done = bf16[32,12288]{1,0:T(8,128)(2,1)} async-done(((bf16[128,12288]{1,0:T(8,128)(2,1)}), bf16[32,12288]{1,0:T(8,128)(2,1)}) %reduce-scatter.5.cloned.1.call-update) | async-done | bytes 786448 | tf_op jit(solution)/shard_map/reduce_scatter | solution.py:59
  531.6 63.1 %reduce-scatter.9.cloned.1.call-done = bf16[32,12288]{1,0:T(8,128)(2,1)} async-done(((bf16[128,12288]{1,0:T(8,128)(2,1)}), bf16[32,12288]{1,0:T(8,128)(2,1)}) %reduce-scatter.9.cloned.1.call-update) | async-done | bytes 786448 | tf_op jit(solution)/shard_map/reduce_scatter | solution.py:70
  602.3 28.7 %collective-permute-done = bf16[32,12288]{1,0:T(8,128)(2,1)} collective-permute-done((bf16[32,12288]{1,0:T(8,128)(2,1)}, bf16[32,12288]{1,0:T(8,128)(2,1)}, u32[]{:S(2)}, u32[]{:S(2)}) %collective-permute-start) | collective-permute-done | bytes 786464 | tf_op jit(solution)/shard_map/ppermute | solution.py:84
  631.0 26.1 %collective-permute-start.2 = (bf16[32,12288]{1,0:T(8,128)(2,1)}, bf16[32,12288]{1,0:T(8,128)(2,1)}, u32[]{:S(2)}, u32[]{:S(2)}) collective-permute-start(bf16[32,12288]{1,0:T(8,128)(2,1)} %collective-permute-done), channel_id=1, source_target_pairs={{0,2},{2,4},{4,6},{6,0},{1,3},{3,5},{5,7},{7,1},{8,10},{10,12},{12... | collective-permute-start | bytes 2359304 | tf_op jit(solution)/shard_map/ppermute | solution.py:84
  661.8 26.8 %dynamic_update_slice.12 = bf16[128,12288]{0,1:T(8,128)(2,1)} dynamic-update-slice(bf16[128,12288]{0,1:T(8,128)(2,1)} %broadcast_in_dim.9, bf16[32,12288]{0,1:T(8,128)(2,1)S(1)} %copy.12, s32[]{:T(128)S(6)} %select_n.42, s32[]{:T(128)} %constant.58.clone.1) | dynamic-update-slice | bytes 1572868 | tf_op jit(solution)/shard_map/dynamic_update_slice | solution.py:80
  691.5 31.8 %dynamic_update_slice.13 = bf16[128,12288]{0,1:T(8,128)(2,1)} dynamic-update-slice(bf16[128,12288]{0,1:T(8,128)(2,1)} %dynamic_update_slice.12, bf16[32,12288]{0,1:T(8,128)(2,1)S(1)} %copy.13, s32[]{:T(128)S(6)} %select_n.44, s32[]{:T(128)} %constant.58.clone.1) | dynamic-update-slice | bytes 1572868 | tf_op jit(solution)/shard_map/dynamic_update_slice | solution.py:85
  726.2 31.8 %dynamic_update_slice.14 = bf16[128,12288]{0,1:T(8,128)(2,1)} dynamic-update-slice(bf16[128,12288]{0,1:T(8,128)(2,1)} %dynamic_update_slice.13, bf16[32,12288]{0,1:T(8,128)(2,1)S(1)} %copy.14, s32[]{:T(128)S(6)} %select_n.46, s32[]{:T(128)} %constant.58.clone.1) | dynamic-update-slice | bytes 1572868 | tf_op jit(solution)/shard_map/dynamic_update_slice | solution.py:90
  760.9 31.8 %dynamic_update_slice.15 = bf16[128,12288]{0,1:T(8,128)(2,1)} dynamic-update-slice(bf16[128,12288]{0,1:T(8,128)(2,1)} %dynamic_update_slice.14, bf16[32,12288]{0,1:T(8,128)(2,1)S(1)} %copy.15, s32[]{:T(128)S(6)} %select_n.48, s32[]{:T(128)} %constant.58.clone.1) | dynamic-update-slice | bytes 1572868 | tf_op jit(solution)/shard_map/dynamic_update_slice | solution.py:85
  792.8 19.2 %convolution_convert_fusion.2 = bf16[128,1536]{1,0:T(8,128)(2,1)} fusion(bf16[128,12288]{0,1:T(8,128)(2,1)} %dynamic_update_slice.15, bf16[1536,12288]{1,0:T(8,128)(2,1)} %all-gather.8.cloned.1.call-done), kind=kOutput, calls=%fused_computation.11 | convolution fusion | flops 4832034816 | bytes 41287680 | tf_op jit(solution)/shard_map/dot_general | solution.py:25
  812.7 4.7 all-to-all-start
  817.5 16.4 %convolution_convert_fusion.3 = bf16[128,1536]{1,0:T(8,128)(2,1)} fusion(bf16[128,12288]{1,0:T(8,128)(2,1)} %all-gather.10.cloned.1.call-done, bf16[12288,1536]{1,0:T(8,128)(2,1)} %all-gather.12.cloned.1.call-done), kind=kOutput, calls=%fused_computation.12 | convolution fusion | flops 4832034816 | bytes 41287680 | tf_op jit(solution)/shard_map/dot_general | solution.py:64
  836.5 26.2 %all-to-all-done = bf16[128,4,3072]{0,2,1:T(8,128)(2,1)} async-done(((bf16[128,4,3072]{0,2,1:T(8,128)(2,1)}), bf16[128,4,3072]{0,2,1:T(8,128)(2,1)}, u32[]{:S(2)}, u32[]{:S(2)}) %all-to-all-start) | async-done | bytes 3145760 | tf_op jit(solution)/shard_map/all_to_all | solution.py:103
  862.8 4.1 all-to-all-start.1
  868.6 4.6 copy.16
  873.3 11.4 %convolution_bitcast_fusion = f32[1536,3072]{0,1:T(8,128)} fusion(bf16[512,3072]{1,0:T(8,128)(2,1)} %bitcast.43, bf16[1,512,1536]{2,1,0:T(8,128)(2,1)} %all-gather.16.cloned.1.call-done), kind=kOutput, calls=%fused_computation.2 | convolution fusion | flops 4831838208 | bytes 23592960 | tf_op jit(solution)/shard_map/dot_general | solution.py:31
  884.7 18.7 %copy.18 = f32[1536,3072]{1,0:T(8,128)} copy(f32[1536,3072]{0,1:T(8,128)} %convolution_bitcast_fusion) | data formatting | bytes 37748736
  905.0 6.9 all-to-all-done.1
  911.9 10.9 %fusion.19 = f32[3072,1536]{1,0:T(8,128)} fusion(bf16[512,3072]{1,0:T(8,128)(2,1)S(1)} %bitcast.42, bf16[512,1536]{1,0:T(8,128)(2,1)} %all-gather.14.cloned.1.call-done), kind=kOutput, calls=%fused_computation.41 | convolution fusion | flops 4831838208 | bytes 23592960 | tf_op jit(solution)/shard_map/dot_general | solution.py:31
  (55 shorter events, 31.6 us)
Async XLA Ops:
  7.2 232.3 %all-gather.8.cloned.1.call-start = ((), (), s32[]{:S(2)}) async-start(), calls=%async_computation.6 | async-start | bytes 47185920 | tf_op jit(solution)/shard_map/all_gather | solution.py:56
  7.9 0.9 copy-start.5
  7.9 460.3 %all-gather.12.cloned.1.call-start = ((), (), s32[]{:S(2)}) async-start(), calls=%async_computation.9 | async-start | bytes 47185920 | tf_op jit(solution)/shard_map/all_gather | solution.py:57
  8.7 522.9 %reduce-scatter.5.cloned.1.call-start = ((), (), s32[]{:S(2)}) async-start(), calls=%async_computation.7 | async-start | bytes 3932160 | tf_op jit(solution)/shard_map/reduce_scatter | solution.py:59
  17.4 242.3 %copy-start.1 = (bf16[1,128,1536]{2,1,0:T(8,128)(2,1)}, bf16[1,128,1536]{2,1,0:T(8,128)(2,1)S(1)}, u32[]{:S(2)}) copy-start(bf16[1,128,1536]{2,1,0:T(8,128)(2,1)S(1)} %all-gather) | copy-start | bytes 1179652
  259.6 0.7 copy-start.7
  259.6 2.6 copy-start.3
  259.7 335.0 %reduce-scatter.9.cloned.1.call-start = ((), (), s32[]{:S(2)}) async-start(), calls=%async_computation.11 | async-start | bytes 3932160 | tf_op jit(solution)/shard_map/reduce_scatter | solution.py:70
  270.1 218.0 %copy-start.2 = (bf16[128,1536]{1,0:T(8,128)(2,1)}, bf16[128,1536]{1,0:T(8,128)(2,1)S(1)}, u32[]{:S(2)}) copy-start(bf16[128,1536]{1,0:T(8,128)(2,1)S(1)} %all_gather.25) | copy-start | bytes 1179652
  488.0 329.4 %all-gather.10.cloned.1.call-start = ((), (), s32[]{:S(2)}) async-start(), calls=%async_computation.8 | async-start | bytes 3932160 | tf_op jit(solution)/shard_map/all_gather | solution.py:63
  598.3 268.5 %reduce-scatter.11.cloned.1.call-start = ((), (), s32[]{:S(2)}) async-start(), calls=%async_computation.12 | async-start | bytes 589824 | tf_op jit(solution)/shard_map/reduce_scatter | solution.py:94
  598.4 32.6 %collective-permute-start = (bf16[32,12288]{1,0:T(8,128)(2,1)}, bf16[32,12288]{1,0:T(8,128)(2,1)}, u32[]{:S(2)}, u32[]{:S(2)}) collective-permute-start(bf16[32,12288]{1,0:T(8,128)(2,1)} %get-tuple-element.18), channel_id=1, source_target_pairs={{0,2},{2,4},{4,6},{6,0},{1,3},{3,5},{5,7},{7,1},{8,10},{10,12},{12... | collective-permute-start | bytes 2359304 | tf_op jit(solution)/shard_map/ppermute | solution.py:84
  599.3 124.0 %collective-permute-start.1 = (bf16[32,12288]{1,0:T(8,128)(2,1)}, bf16[32,12288]{1,0:T(8,128)(2,1)}, u32[]{:S(2)}, u32[]{:S(2)}) collective-permute-start(bf16[32,12288]{1,0:T(8,128)(2,1)} %get-tuple-element.18), channel_id=1, source_target_pairs={{0,6},{2,0},{4,2},{6,4},{1,7},{3,1},{5,3},{7,5},{8,14},{10,8},{12,... | collective-permute-start | bytes 2359304 | tf_op jit(solution)/shard_map/ppermute | solution.py:89
  631.0 127.1 %collective-permute-start.2 = (bf16[32,12288]{1,0:T(8,128)(2,1)}, bf16[32,12288]{1,0:T(8,128)(2,1)}, u32[]{:S(2)}, u32[]{:S(2)}) collective-permute-start(bf16[32,12288]{1,0:T(8,128)(2,1)} %collective-permute-done), channel_id=1, source_target_pairs={{0,2},{2,4},{4,6},{6,0},{1,3},{3,5},{5,7},{7,1},{8,10},{10,12},{12... | collective-permute-start | bytes 2359304 | tf_op jit(solution)/shard_map/ppermute | solution.py:84
  812.0 61.3 %all-gather.16.cloned.1.call-start = ((), (), s32[]{:S(2)}) async-start(), calls=%async_computation.14 | async-start | bytes 1966080 | tf_op jit(solution)/shard_map/all_gather | solution.py:99
  812.7 50.1 %all-to-all-start = ((bf16[128,4,3072]{0,2,1:T(8,128)(2,1)}), bf16[128,4,3072]{0,2,1:T(8,128)(2,1)}, u32[]{:S(2)}, u32[]{:S(2)}) async-start(bf16[128,4,3072]{0,2,1:T(8,128)(2,1)} %bitcast.5), calls=%async_computation.4 | async-start | bytes 6291456 | tf_op jit(solution)/shard_map/all_to_all | solution.py:103
  817.4 86.0 %reduce-scatter.7.cloned.1.call-start = ((), (), s32[]{:S(2)}) async-start(), calls=%async_computation.10 | async-start | bytes 589824 | tf_op jit(solution)/shard_map/reduce_scatter | solution.py:65
  817.5 17.2 %copy-start = (bf16[128,12288]{1,0:T(8,128)(2,1)S(1)}, bf16[128,12288]{1,0:T(8,128)(2,1)}, u32[]{:S(2)}) copy-start(bf16[128,12288]{1,0:T(8,128)(2,1)} %all-gather.10.cloned.1.call-done) | copy-start | bytes 9437188
  833.9 71.1 %all-gather.14.cloned.1.call-start = ((), (), s32[]{:S(2)}) async-start(), calls=%async_computation.13 | async-start | bytes 1966080 | tf_op jit(solution)/shard_map/all_gather | solution.py:100
  862.8 4.1 copy-start.4
  862.8 49.1 %all-to-all-start.1 = ((bf16[128,4,3072]{2,0,1:T(8,128)(2,1)}), bf16[128,4,3072]{2,0,1:T(8,128)(2,1)S(1)}, u32[]{:S(2)}, u32[]{:S(2)}) async-start(bf16[128,4,3072]{2,0,1:T(8,128)(2,1)} %bitcast.41), calls=%async_computation.5 | async-start | bytes 6291456 | tf_op jit(solution)/shard_map/all_to_all | solution.py:104
  884.7 18.7 %copy-start.6 = (bf16[1,64,1536]{2,1,0:T(8,128)(2,1)S(1)}, bf16[1,64,1536]{2,1,0:T(8,128)(2,1)}, u32[]{:S(2)}) copy-start(bf16[1,64,1536]{2,1,0:T(8,128)(2,1)} %param.5) | copy-start | bytes 589828
Sparse Core Ops, SparseCore 0:
  9.5 229.8 all-gather.7
  241.0 227.1 all-gather.11
  471.1 60.3 reduce-scatter.4
  534.3 60.3 reduce-scatter.8
  598.5 105.4 all-gather.9
  812.1 14.2 reduce-scatter.10
  827.9 28.1 all-gather.15
  858.4 12.2 reduce-scatter.6
  872.2 28.1 all-gather.13
